TPU v7x, 256 devices: a whole 4x4x8 slice. The times are simulated.
256 devices in a mesh: adapter: 64 (over x, z, core), tensor: 4 (over y).
Axes of the slice: x: 4, y: 4, z: 8, core: 2. Of those that a mesh axis runs over, the one named last changes fastest.
Arguments:
- activations: bfloat16 [32768, 4096], P('adapter', 'tensor'), may hold values from -6 to 6
- output_gradient: bfloat16 [32768, 4096], P('adapter', 'tensor'), may hold values from -6 to 6
- frozen_weight: bfloat16 [4096, 4096], P(None, 'tensor'), may hold values from -0.09375 to 0.09375
- adapter_down_weight: bfloat16 [8192, 4096], P('adapter', 'tensor'), may hold values from -0.09375 to 0.09375
- adapter_up_weight: bfloat16 [8192, 4096], P('adapter', 'tensor'), may hold values from -0.09375 to 0.09375
- adapter_slot_table: int32 [512], replicated, may hold values from 0 to 511, as said below
- group_adapter_index: int32 [64, 48], P('adapter'), may hold values from 0 to 511, as said below
- group_token_length: int32 [64, 48], P('adapter'), may hold values from 1 to 16, as said below
Outputs:
- input_gradient: bfloat16 [32768, 4096], P('adapter', 'tensor')
- down_grad: float32 [8192, 4096], P('adapter', 'tensor')
- up_grad: float32 [8192, 4096], P('adapter', 'tensor')
Inputs may be any that keep to these rules, and one draw needn't show every extreme that they name: `adapter_slot_table`: a permutation of the slots; slot k lies on adapter index k // 8. `group_adapter_index`: the adapters of one index's groups lie on distinct indices of the adapter axis; on every index one group of exactly 16 tokens uses an adapter stored on one index that is the same for all indices. `group_token_length`: each row sums to 512 and holds a group of exactly 16 tokens.
All inputs are finite; a program needn't handle non-finite values.
Results may differ from a plain program's by a relative error of at most 0.015.
Values may be sent and summed in bfloat16 or wider, within the bound.
A program may use at most 128 MiB of HBM per device.

v0:
```python
import jax
import jax.numpy as jnp
from jax import lax
from jax.sharding import PartitionSpec as P

ADAPTER_RANK = 16
ADP_DEV = 8
adapter_scale = 2.0


def rank_sums(down_part, up_part):
    return (
        lax.psum(down_part.astype(jnp.bfloat16), "tensor").astype(jnp.float32),
        lax.psum(up_part.astype(jnp.bfloat16), "tensor").astype(jnp.float32),
    )


def widen(mask, values):
    return jnp.where(mask[:, :, None], values[:, None, :], jnp.zeros((), values.dtype)).reshape(
        values.shape[0], mask.shape[1] * values.shape[1]
    )


def narrow(wide, mask):
    shaped = wide.reshape(wide.shape[0], mask.shape[1], ADAPTER_RANK)
    return jnp.sum(shaped * mask[:, :, None].astype(jnp.float32), axis=1)


def on_device(
    activations,
    output_gradient,
    frozen_weight,
    adapter_down_weight,
    adapter_up_weight,
    adapter_slot_table,
    group_adapter_index,
    group_token_length,
):
    tok_rows = activations.shape[0]
    devices = lax.axis_size("adapter")
    own_index = lax.axis_index("adapter")
    adapter_count = adapter_slot_table.shape[0]
    lengths = group_token_length[0]
    matched = group_adapter_index[0][:, None] == jnp.arange(adapter_count, dtype=jnp.int32)[None, :]
    group_slot = jnp.sum(jnp.where(matched, adapter_slot_table[None, :], 0), axis=1)
    group_owner = group_slot // ADP_DEV
    group_end = jnp.cumsum(lengths)
    positions = jnp.arange(tok_rows, dtype=jnp.int32)
    tok_group = jnp.sum((positions[:, None] >= group_end[None, :]).astype(jnp.int32), axis=1)
    group_onehot = tok_group[:, None] == jnp.arange(lengths.shape[0], dtype=jnp.int32)[None, :]
    tok_owner = jnp.sum(jnp.where(group_onehot, group_owner[None, :], 0), axis=1)
    gathered = lax.all_gather(jnp.stack([group_slot, lengths])[None], "adapter", axis=0, tiled=True)
    from_mine = gathered[:, 0] // ADP_DEV == own_index
    source_count = jnp.sum(jnp.where(from_mine, gathered[:, 1], 0), axis=1)
    source_local = jnp.sum(jnp.where(from_mine, gathered[:, 0] % ADP_DEV, 0), axis=1)
    source_hot = (source_local[:, None] == jnp.arange(ADP_DEV, dtype=jnp.int32)[None, :]) & (
        source_count > 0
    )[:, None]
    eye_rank = jnp.eye(ADAPTER_RANK, dtype=bool)
    selector = (source_hot[:, None, :, None] & eye_rank[None, :, None, :]).reshape(
        devices * ADAPTER_RANK, ADP_DEV * ADAPTER_RANK
    )
    selected_reduced = selector.astype(jnp.bfloat16)
    outgoing_down = jnp.dot(
        selected_reduced, adapter_down_weight, preferred_element_type=jnp.float32
    ).astype(jnp.bfloat16)
    outgoing_up = jnp.dot(
        selected_reduced, adapter_up_weight, preferred_element_type=jnp.float32
    ).astype(jnp.bfloat16)
    received_down, got_up = (
        lax.all_to_all(outgoing_down, "adapter", split_axis=0, concat_axis=0, tiled=True),
        lax.all_to_all(outgoing_up, "adapter", split_axis=0, concat_axis=0, tiled=True),
    )
    owner_hot = tok_owner[:, None] == jnp.arange(devices, dtype=jnp.int32)[None, :]
    down_wide = lax.dot_general(
        activations, received_down, (((1,), (1,)), ((), ())), preferred_element_type=jnp.float32
    )
    up_wide = lax.dot_general(
        output_gradient, got_up, (((1,), (1,)), ((), ())), preferred_element_type=jnp.float32
    )
    down_proj, up_proj = rank_sums(narrow(down_wide, owner_hot), narrow(up_wide, owner_hot))
    down_spread = widen(owner_hot, down_proj.astype(jnp.bfloat16))
    up_broadcast = widen(owner_hot, up_proj.astype(jnp.bfloat16))
    adapter_term = (
        adapter_scale * jnp.dot(up_broadcast, received_down, preferred_element_type=jnp.float32)
    ).astype(jnp.bfloat16)
    partial_down = adapter_scale * lax.dot_general(
        up_broadcast, activations, (((0,), (0,)), ((), ())), preferred_element_type=jnp.float32
    )
    partial_up = adapter_scale * lax.dot_general(
        down_spread, output_gradient, (((0,), (0,)), ((), ())), preferred_element_type=jnp.float32
    )
    back_down, back_up = (
        lax.all_to_all(
            partial_down.astype(jnp.bfloat16), "adapter", split_axis=0, concat_axis=0, tiled=True
        ).astype(partial_down.dtype),
        lax.all_to_all(
            partial_up.astype(jnp.bfloat16), "adapter", split_axis=0, concat_axis=0, tiled=True
        ).astype(partial_up.dtype),
    )
    select_full = selector.astype(jnp.float32)
    down_grad = lax.dot_general(
        select_full,
        back_down,
        (((0,), (0,)), ((), ())),
        precision=lax.Precision.HIGHEST,
        preferred_element_type=jnp.float32,
    )
    up_grad = lax.dot_general(
        select_full,
        back_up,
        (((0,), (0,)), ((), ())),
        precision=lax.Precision.HIGHEST,
        preferred_element_type=jnp.float32,
    )
    frozen_total_sum = lax.psum_scatter(
        lax.dot_general(
            frozen_weight,
            output_gradient,
            (((1,), (1,)), ((), ())),
            preferred_element_type=jnp.float32,
        ).astype(jnp.bfloat16),
        "tensor",
        scatter_dimension=0,
        tiled=True,
    ).astype(jnp.float32)
    input_gradient = (frozen_total_sum.T + adapter_term.astype(jnp.float32)).astype(jnp.bfloat16)
    return (input_gradient, down_grad, up_grad)


def solution(mesh):
    in_specs = (
        P("adapter", "tensor"),
        P("adapter", "tensor"),
        P(None, "tensor"),
        P("adapter", "tensor"),
        P("adapter", "tensor"),
        P(),
        P("adapter", None),
        P("adapter", None),
    )
    out_specs = (P("adapter", "tensor"), P("adapter", "tensor"), P("adapter", "tensor"))
    return jax.shard_map(
        on_device, mesh=mesh, in_specs=in_specs, out_specs=out_specs, check_vma=False
    )
```

profile of v0, /device:TPU:1, one launch (start us, length us, event | category | flops | bytes accessed | tf_op | source)
XLA Modules:
  0.0 331.1 jit_solution(9683461043637806220)
XLA Ops:
  7.2 0.0 copy-start
  7.2 0.0 copy-start.4
  7.2 1.0 select_reduce_fusion.1
  8.2 0.7 add_bitcast_fusion
  8.8 48.1 %all-gather.1 = s32[64,2,48]{2,1,0:T(2,128)S(1)} all-gather(s32[1,2,48]{2,1,0:T(2,128)S(1)} %add_bitcast_fusion), channel_id=2, replica_groups=mesh['adapter'=64,'tensor'=4] {'adapter'}, dimensions={0}, use_global_device_ids=true | all-gather | bytes 24960 | tf_op jit(solution)/shard_map/all_gather | solution.py:52
  57.0 0.1 fusion.10
  57.1 0.1 select_reduce_fusion.2
  57.2 0.1 fusion.6
  57.3 0.5 broadcast_and_fusion
  57.8 1.5 and.72
  59.3 0.0 copy-done.4
  59.3 2.0 convolution_convert_fusion.1
  61.3 0.0 copy-start.5
  61.3 6.6 %all-to-all-start.1 = ((bf16[64,16,1024]{2,1,0:T(8,128)(2,1)}), bf16[64,16,1024]{2,1,0:T(8,128)(2,1)S(1)}, u32[]{:S(2)}, u32[]{:S(2)}) async-start(bf16[64,16,1024]{2,1,0:T(8,128)(2,1)} %bitcast.11), calls=%async_computation.2 | async-start | bytes 4194304 | tf_op jit(solution)/shard_map/all_to_all | solution.py:71
  67.9 0.0 copy-done.5
  67.9 2.0 convolution_convert_fusion.2
  70.0 49.2 %all-to-all-done.1 = bf16[64,16,1024]{2,1,0:T(8,128)(2,1)S(1)} async-done(((bf16[64,16,1024]{2,1,0:T(8,128)(2,1)}), bf16[64,16,1024]{2,1,0:T(8,128)(2,1)S(1)}, u32[]{:S(2)}, u32[]{:S(2)}) %all-to-all-start.1) | async-done | bytes 2097184 | tf_op jit(solution)/shard_map/all_to_all | solution.py:71
  119.2 0.0 copy-start.1
  119.2 6.1 %all-to-all-start = ((bf16[64,16,1024]{2,1,0:T(8,128)(2,1)}), bf16[64,16,1024]{2,1,0:T(8,128)(2,1)}, u32[]{:S(2)}, u32[]{:S(2)}) async-start(bf16[64,16,1024]{2,1,0:T(8,128)(2,1)} %bitcast.7), calls=%async_computation.1 | async-start | bytes 4194304 | tf_op jit(solution)/shard_map/all_to_all | solution.py:72
  125.3 0.0 copy-done.6
  125.3 0.1 copy.27
  125.4 0.1 reduce-window.8
  125.5 0.1 reduce
  125.6 0.1 convert_reduce_fusion
  125.7 0.1 select_reduce_fusion
  125.9 0.0 copy-done.1
  125.9 3.9 %fusion.13 = f32[1024,512]{1,0:T(8,128)} fusion(bf16[1024,1024]{1,0:T(8,128)(2,1)S(1)} %bitcast.57, bf16[512,1024]{1,0:T(8,128)(2,1)} %param.8), kind=kOutput, calls=%fused_computation.47 | convolution fusion | flops 1073741824 | bytes 5242880 | tf_op jit(solution)/shard_map/dot_general | solution.py:75
  129.7 46.8 %all-to-all-done = bf16[64,16,1024]{2,1,0:T(8,128)(2,1)} async-done(((bf16[64,16,1024]{2,1,0:T(8,128)(2,1)}), bf16[64,16,1024]{2,1,0:T(8,128)(2,1)}, u32[]{:S(2)}, u32[]{:S(2)}) %all-to-all-start) | async-done | bytes 2097184 | tf_op jit(solution)/shard_map/all_to_all | solution.py:72
  176.5 0.0 copy-done
  176.5 3.0 fusion.11
  179.5 0.0 copy-done.3
  179.5 0.7 multiply_reduce_fusion
  180.2 13.6 %all-reduce = (bf16[512,16]{0,1:T(8,128)(2,1)S(1)}, bf16[512,16]{0,1:T(8,128)(2,1)S(1)}) all-reduce(bf16[512,16]{0,1:T(8,128)(2,1)S(1)} %get-tuple-element.16, bf16[512,16]{0,1:T(8,128)(2,1)S(1)} %get-tuple-element.15), channel_id=1, replica_groups=mesh['adapter'=64,'tensor'=4] {'tensor'}, use_global_device_ids=true, to_apply=%region_8.9 | all-reduce | flops 16384 | bytes 65536 | tf_op jit(solution)/shard_map/psum | solution.py:14
  193.8 1.2 broadcast_select_fusion
  195.0 2.6 multiply_convert_fusion
  197.6 9.6 %all-to-all-start.3 = ((bf16[64,16,1024]{2,1,0:T(8,128)(2,1)}), bf16[64,16,1024]{2,1,0:T(8,128)(2,1)S(1)}, u32[]{:S(2)}, u32[]{:S(2)}) async-start(bf16[64,16,1024]{2,1,0:T(8,128)(2,1)} %bitcast.58), calls=%async_computation.4 | async-start | bytes 4194304 | tf_op jit(solution)/shard_map/all_to_all | solution.py:97
  207.2 0.2 reduce-scatter.2.cloned.1.call-start
  207.4 9.6 %convolution_convert_fusion = bf16[4096,512]{1,0:T(8,128)(2,1)} fusion(bf16[4096,1024]{1,0:T(8,128)(2,1)} %param.10, bf16[512,1024]{1,0:T(8,128)(2,1)S(1)} %copy-done), kind=kOutput, calls=%fused_computation | convolution fusion | flops 4297064448 | bytes 13631488 | tf_op jit(solution)/shard_map/dot_general | solution.py:117
  217.0 0.0 reduce-scatter.2.cloned.1.call-update
  217.0 4.2 %multiply_convert_fusion.1 = bf16[1024,1024]{1,0:T(8,128)(2,1)} fusion(bf16[512,1024]{0,1:T(8,128)(2,1)} %bitcast.62, bf16[512,1024]{1,0:T(8,128)(2,1)} %param.8), kind=kOutput, calls=%fused_computation.2 | convolution fusion | flops 1075838976 | bytes 4194304 | tf_op jit(solution)/shard_map/dot_general | solution.py:87
  221.2 37.2 %all-to-all-done.3 = bf16[64,16,1024]{2,1,0:T(8,128)(2,1)S(1)} async-done(((bf16[64,16,1024]{2,1,0:T(8,128)(2,1)}), bf16[64,16,1024]{2,1,0:T(8,128)(2,1)S(1)}, u32[]{:S(2)}, u32[]{:S(2)}) %all-to-all-start.3) | async-done | bytes 2097184 | tf_op jit(solution)/shard_map/all_to_all | solution.py:97
  258.4 6.0 %all-to-all-start.2 = ((bf16[64,16,1024]{2,1,0:T(8,128)(2,1)}), bf16[64,16,1024]{2,1,0:T(8,128)(2,1)}, u32[]{:S(2)}, u32[]{:S(2)}) async-start(bf16[64,16,1024]{2,1,0:T(8,128)(2,1)} %bitcast.59), calls=%async_computation.3 | async-start | bytes 4194304 | tf_op jit(solution)/shard_map/all_to_all | solution.py:94
  264.4 1.3 fusion.14
  265.7 49.9 %all-to-all-done.2 = bf16[64,16,1024]{2,1,0:T(8,128)(2,1)} async-done(((bf16[64,16,1024]{2,1,0:T(8,128)(2,1)}), bf16[64,16,1024]{2,1,0:T(8,128)(2,1)}, u32[]{:S(2)}, u32[]{:S(2)}) %all-to-all-start.2) | async-done | bytes 2097184 | tf_op jit(solution)/shard_map/all_to_all | solution.py:94
  315.6 2.9 fusion.12
  318.5 0.0 copy-done.2
  318.5 3.5 %fusion.1 = bf16[512,1024]{0,1:T(8,128)(2,1)} fusion(bf16[1024,512]{1,0:T(8,128)(2,1)} %reduce-scatter.2.cloned.1.call-done, bf16[64,16,1024]{2,1,0:T(8,128)(2,1)S(1)} %copy-done.2, pred[512,64]{0,1:T(8,128)(4,1)S(1)} %get-tuple-element.26, bf16[512,16]{0,1:T(8,128)(2,1)S(1)} %get-tuple-element.19), kind=kOutput, calls=%fused_computation.6 | convolution fusion | flops 1077411840 | bytes 4243456 | tf_op jit(solution)/shard_map/dot_general | solution.py:85
  322.0 2.3 copy.30
  (8 shorter events, 0.1 us)
Async XLA Ops:
  7.2 169.3 %copy-start = (bf16[512,1024]{1,0:T(8,128)(2,1)S(1)}, bf16[512,1024]{1,0:T(8,128)(2,1)}, u32[]{:S(2)}) copy-start(bf16[512,1024]{1,0:T(8,128)(2,1)} %param.9) | copy-start | bytes 3145732
  7.2 52.1 %copy-start.4 = (bf16[128,1024]{1,0:T(8,128)(2,1)S(1)}, bf16[128,1024]{1,0:T(8,128)(2,1)}, u32[]{:S(2)}) copy-start(bf16[128,1024]{1,0:T(8,128)(2,1)} %param.11) | copy-start | bytes 786436
  61.3 6.6 %copy-start.5 = (bf16[128,1024]{1,0:T(8,128)(2,1)S(1)}, bf16[128,1024]{1,0:T(8,128)(2,1)}, u32[]{:S(2)}) copy-start(bf16[128,1024]{1,0:T(8,128)(2,1)} %param.12) | copy-start | bytes 786436
  61.3 57.8 %all-to-all-start.1 = ((bf16[64,16,1024]{2,1,0:T(8,128)(2,1)}), bf16[64,16,1024]{2,1,0:T(8,128)(2,1)S(1)}, u32[]{:S(2)}, u32[]{:S(2)}) async-start(bf16[64,16,1024]{2,1,0:T(8,128)(2,1)} %bitcast.11), calls=%async_computation.2 | async-start | bytes 4194304 | tf_op jit(solution)/shard_map/all_to_all | solution.py:71
  119.2 6.7 %copy-start.1 = (bf16[64,16,1024]{2,1,0:T(8,128)(2,1)}, bf16[64,16,1024]{2,1,0:T(8,128)(2,1)S(1)}, u32[]{:S(2)}) copy-start(bf16[64,16,1024]{2,1,0:T(8,128)(2,1)S(1)} %all-to-all-done.1) | copy-start | bytes 6291460
  119.2 6.1 %copy-start.6 = (s32[1,48]{1,0:T(1,128)S(1)}, s32[1,48]{1,0:T(1,128)}, u32[]{:S(2)}) copy-start(s32[1,48]{1,0:T(1,128)} %param.15) | copy-start | bytes 580
  119.2 57.3 %all-to-all-start = ((bf16[64,16,1024]{2,1,0:T(8,128)(2,1)}), bf16[64,16,1024]{2,1,0:T(8,128)(2,1)}, u32[]{:S(2)}, u32[]{:S(2)}) async-start(bf16[64,16,1024]{2,1,0:T(8,128)(2,1)} %bitcast.7), calls=%async_computation.1 | async-start | bytes 4194304 | tf_op jit(solution)/shard_map/all_to_all | solution.py:72
  176.5 3.0 copy-start.3
  197.6 60.8 %all-to-all-start.3 = ((bf16[64,16,1024]{2,1,0:T(8,128)(2,1)}), bf16[64,16,1024]{2,1,0:T(8,128)(2,1)S(1)}, u32[]{:S(2)}, u32[]{:S(2)}) async-start(bf16[64,16,1024]{2,1,0:T(8,128)(2,1)} %bitcast.58), calls=%async_computation.4 | async-start | bytes 4194304 | tf_op jit(solution)/shard_map/all_to_all | solution.py:97
  207.2 111.3 %reduce-scatter.2.cloned.1.call-start = ((), (), s32[]{:S(2)}) async-start(), calls=%async_computation.5 | async-start | bytes 5242880 | tf_op jit(solution)/shard_map/reduce_scatter | solution.py:116
  258.4 57.2 %all-to-all-start.2 = ((bf16[64,16,1024]{2,1,0:T(8,128)(2,1)}), bf16[64,16,1024]{2,1,0:T(8,128)(2,1)}, u32[]{:S(2)}, u32[]{:S(2)}) async-start(bf16[64,16,1024]{2,1,0:T(8,128)(2,1)} %bitcast.59), calls=%async_computation.3 | async-start | bytes 4194304 | tf_op jit(solution)/shard_map/all_to_all | solution.py:94
  265.7 52.8 %copy-start.2 = (bf16[64,16,1024]{2,1,0:T(8,128)(2,1)S(1)}, bf16[64,16,1024]{2,1,0:T(8,128)(2,1)}, u32[]{:S(2)}) copy-start(bf16[64,16,1024]{2,1,0:T(8,128)(2,1)} %copy-done.1) | copy-start | bytes 6291460
Sparse Core Ops, SparseCore 0:
  217.1 48.8 reduce-scatter.1
where the time goes:
time: 332 us; the launch traced here: 331 us
  waiting for transfers between devices  183 us (55%)
  blocking collectives  61.7 us (19%)
  matrix products  35 us (11%)
  starting transfers between devices  28.5 us (9%)
  between operations  14.2 us (4%)
  other arithmetic  4.68 us (1%)
  local copies, waits for them, and re-layouts  3.91 us (1%)
    all_to_all x1, waiting for transfers between devices, on_device(): lax.all_to_all(partial_down.astype(jnp.bfloat16), 'adapter', split_axis=0...  49.9 us
    all_to_all x1, waiting for transfers between devices, on_device(): lax.all_to_all(outgoing_down, 'adapter', split_axis=0, concat_axis=0, til...  49.2 us
    all_gather x1, blocking collectives, on_device(): lax.all_gather(jnp.stack([group_slot, lengths])[None], 'adapter', axis=0,...  48.1 us
    all_to_all x1, waiting for transfers between devices, on_device(): lax.all_to_all(outgoing_up, 'adapter', split_axis=0, concat_axis=0, tiled...  46.8 us
    all_to_all x1, waiting for transfers between devices, on_device(): lax.all_to_all(partial_up.astype(jnp.bfloat16), 'adapter', split_axis=0,...  37.2 us
    psum x1, blocking collectives, rank_sums(): lax.psum(up_part.astype(jnp.bfloat16), 'tensor').astype(jnp.float32)  13.6 us
    all_to_all x1, starting transfers between devices, on_device(): lax.all_to_all(partial_up.astype(jnp.bfloat16), 'adapter', split_axis=0,...  9.57 us
    dot_general x1, matrix products, on_device(): lax.dot_general(frozen_weight, output_gradient, (((1,), (1,)), ((), ())),...  9.56 us
  transfers between devices with their start and end apart: 5, of which 4 were waited for; matrix products, arithmetic and copies ran while one was open for 7% of the time, Pallas kernels for 0%

commit v1 on v0

--- a/solution.py
+++ b/solution.py
@@ -2,16 +2,21 @@
 import jax.numpy as jnp
 from jax import lax
 from jax.sharding import PartitionSpec as P
+from jax.lax import all_gather
 
 ADAPTER_RANK = 16
 ADP_DEV = 8
 adapter_scale = 2.0
 
 
+def balance_shifts_all_for(mine_x):
+    return jnp.sum(all_gather(mine_x, "tensor"), 0)
+
+
 def rank_sums(down_part, up_part):
     return (
         lax.psum(down_part.astype(jnp.bfloat16), "tensor").astype(jnp.float32),
-        lax.psum(up_part.astype(jnp.bfloat16), "tensor").astype(jnp.float32),
+        balance_shifts_all_for(up_part.astype(jnp.bfloat16)).astype(jnp.float32),
     )
 
 

time: 332 us -> 344 us (1.036)
  blocking collectives: 61.7 us -> 70.8 us
    all_gather x0 -> x1, blocking collectives: none -> 9.49 us  [balance_shifts_all_for(): return jnp.sum(all_gather(mine_x, 'tensor'), 0)]
where the time goes in v1:
time: 344 us; the launch traced here: 343 us
  waiting for transfers between devices  183 us (53%)
  blocking collectives  70.8 us (21%)
  matrix products  35 us (10%)
  starting transfers between devices  31.2 us (9%)
  between operations  14.2 us (4%)
  other arithmetic  4.76 us (1%)
  local copies, waits for them, and re-layouts  3.94 us (1%)
    all_to_all x1, waiting for transfers between devices, on_device(): lax.all_to_all(partial_down.astype(jnp.bfloat16), 'adapter', split_axis=0...  49.9 us
    all_to_all x1, waiting for transfers between devices, on_device(): lax.all_to_all(outgoing_down, 'adapter', split_axis=0, concat_axis=0, til...  49.2 us
    all_gather x1, blocking collectives, on_device(): lax.all_gather(jnp.stack([group_slot, lengths])[None], 'adapter', axis=0,...  48.1 us
    all_to_all x1, waiting for transfers between devices, on_device(): lax.all_to_all(outgoing_up, 'adapter', split_axis=0, concat_axis=0, tiled...  46.8 us
    all_to_all x1, waiting for transfers between devices, on_device(): lax.all_to_all(partial_up.astype(jnp.bfloat16), 'adapter', split_axis=0,...  37.2 us
    psum x1, blocking collectives, rank_sums(): lax.psum(down_part.astype(jnp.bfloat16), 'tensor').astype(jnp.float32)  13.1 us
    all_to_all x1, starting transfers between devices, on_device(): lax.all_to_all(partial_up.astype(jnp.bfloat16), 'adapter', split_axis=0,...  12.2 us
    dot_general x1, matrix products, on_device(): lax.dot_general(frozen_weight, output_gradient, (((1,), (1,)), ((), ())),...  9.56 us
  transfers between devices with their start and end apart: 5, of which 4 were waited for; matrix products, arithmetic and copies ran while one was open for 7% of the time, Pallas kernels for 0%

profile of v1, /device:TPU:1, one launch (start us, length us, event | category | flops | bytes accessed | tf_op | source)
XLA Modules:
  0.0 342.9 jit_solution(701613480540861170)
XLA Ops:
  7.2 0.0 copy-start
  7.2 0.0 copy-start.4
  7.2 1.0 select_reduce_fusion.1
  8.2 0.7 add_bitcast_fusion
  8.8 48.1 %all-gather.2 = s32[64,2,48]{2,1,0:T(2,128)S(1)} all-gather(s32[1,2,48]{2,1,0:T(2,128)S(1)} %add_bitcast_fusion), channel_id=2, replica_groups=mesh['adapter'=64,'tensor'=4] {'adapter'}, dimensions={0}, use_global_device_ids=true | all-gather | bytes 24960 | tf_op jit(solution)/shard_map/all_gather | solution.py:57
  57.0 0.1 fusion.10
  57.1 0.1 select_reduce_fusion.2
  57.2 0.1 fusion.6
  57.3 0.5 broadcast_and_fusion
  57.8 1.5 and.72
  59.3 0.0 copy-done.4
  59.3 2.0 convolution_convert_fusion.1
  61.3 6.6 %all-to-all-start.1 = ((bf16[64,16,1024]{2,1,0:T(8,128)(2,1)}), bf16[64,16,1024]{2,1,0:T(8,128)(2,1)S(1)}, u32[]{:S(2)}, u32[]{:S(2)}) async-start(bf16[64,16,1024]{2,1,0:T(8,128)(2,1)} %bitcast.11), calls=%async_computation.2 | async-start | bytes 4194304 | tf_op jit(solution)/shard_map/all_to_all | solution.py:76
  67.9 0.0 copy-done.5
  67.9 2.0 convolution_convert_fusion.2
  70.0 49.2 %all-to-all-done.1 = bf16[64,16,1024]{2,1,0:T(8,128)(2,1)S(1)} async-done(((bf16[64,16,1024]{2,1,0:T(8,128)(2,1)}), bf16[64,16,1024]{2,1,0:T(8,128)(2,1)S(1)}, u32[]{:S(2)}, u32[]{:S(2)}) %all-to-all-start.1) | async-done | bytes 2097184 | tf_op jit(solution)/shard_map/all_to_all | solution.py:76
  119.2 6.1 %all-to-all-start = ((bf16[64,16,1024]{2,1,0:T(8,128)(2,1)}), bf16[64,16,1024]{2,1,0:T(8,128)(2,1)}, u32[]{:S(2)}, u32[]{:S(2)}) async-start(bf16[64,16,1024]{2,1,0:T(8,128)(2,1)} %bitcast.7), calls=%async_computation.1 | async-start | bytes 4194304 | tf_op jit(solution)/shard_map/all_to_all | solution.py:77
  125.3 0.0 copy-done.6
  125.3 0.1 copy.27
  125.4 0.1 reduce-window.8
  125.5 0.1 reduce.1
  125.6 0.1 convert_reduce_fusion
  125.7 0.1 select_reduce_fusion
  125.9 0.0 copy-done.1
  125.9 3.9 %fusion.13 = f32[1024,512]{1,0:T(8,128)} fusion(bf16[1024,1024]{1,0:T(8,128)(2,1)S(1)} %bitcast.59, bf16[512,1024]{1,0:T(8,128)(2,1)} %param.8), kind=kOutput, calls=%fused_computation.47 | convolution fusion | flops 1073741824 | bytes 5242880 | tf_op jit(solution)/shard_map/dot_general | solution.py:80
  129.7 46.8 %all-to-all-done = bf16[64,16,1024]{2,1,0:T(8,128)(2,1)} async-done(((bf16[64,16,1024]{2,1,0:T(8,128)(2,1)}), bf16[64,16,1024]{2,1,0:T(8,128)(2,1)}, u32[]{:S(2)}, u32[]{:S(2)}) %all-to-all-start) | async-done | bytes 2097184 | tf_op jit(solution)/shard_map/all_to_all | solution.py:77
  176.5 0.0 copy-done
  176.5 3.0 fusion.11
  179.5 0.0 copy-done.3
  179.5 0.7 multiply_reduce_fusion
  180.2 9.5 %all-gather.1 = bf16[2048,16]{0,1:T(8,128)(2,1)S(1)} all-gather(bf16[512,16]{0,1:T(8,128)(2,1)S(1)} %get-tuple-element.16), channel_id=3, replica_groups=mesh['adapter'=64,'tensor'=4] {'tensor'}, dimensions={0}, use_global_device_ids=true | all-gather | bytes 81920 | tf_op jit(solution)/shard_map/all_gather | solution.py:13
  189.7 13.1 %psum.7 = bf16[512,16]{0,1:T(8,128)(2,1)S(1)} all-reduce(bf16[512,16]{0,1:T(8,128)(2,1)S(1)} %get-tuple-element.15), channel_id=1, replica_groups=mesh['adapter'=64,'tensor'=4] {'tensor'}, use_global_device_ids=true, to_apply=%region_10.11 | all-reduce | flops 8192 | bytes 32768 | tf_op jit(solution)/shard_map/psum | solution.py:18
  202.9 0.1 reduce_sum.84
  203.0 1.2 broadcast_select_fusion
  204.1 2.6 multiply_convert_fusion
  206.7 12.2 %all-to-all-start.3 = ((bf16[64,16,1024]{2,1,0:T(8,128)(2,1)}), bf16[64,16,1024]{2,1,0:T(8,128)(2,1)S(1)}, u32[]{:S(2)}, u32[]{:S(2)}) async-start(bf16[64,16,1024]{2,1,0:T(8,128)(2,1)} %bitcast.60), calls=%async_computation.4 | async-start | bytes 4194304 | tf_op jit(solution)/shard_map/all_to_all | solution.py:102
  219.0 0.2 reduce-scatter.2.cloned.1.call-start
  219.2 9.6 %convolution_convert_fusion = bf16[4096,512]{1,0:T(8,128)(2,1)} fusion(bf16[4096,1024]{1,0:T(8,128)(2,1)} %param.10, bf16[512,1024]{1,0:T(8,128)(2,1)S(1)} %copy-done), kind=kOutput, calls=%fused_computation | convolution fusion | flops 4297064448 | bytes 13631488 | tf_op jit(solution)/shard_map/dot_general | solution.py:122
  228.8 0.0 reduce-scatter.2.cloned.1.call-update
  228.8 4.2 %multiply_convert_fusion.1 = bf16[1024,1024]{1,0:T(8,128)(2,1)} fusion(bf16[512,1024]{0,1:T(8,128)(2,1)} %bitcast.64, bf16[512,1024]{1,0:T(8,128)(2,1)} %param.8), kind=kOutput, calls=%fused_computation.2 | convolution fusion | flops 1075838976 | bytes 4194304 | tf_op jit(solution)/shard_map/dot_general | solution.py:92
  233.0 37.2 %all-to-all-done.3 = bf16[64,16,1024]{2,1,0:T(8,128)(2,1)S(1)} async-done(((bf16[64,16,1024]{2,1,0:T(8,128)(2,1)}), bf16[64,16,1024]{2,1,0:T(8,128)(2,1)S(1)}, u32[]{:S(2)}, u32[]{:S(2)}) %all-to-all-start.3) | async-done | bytes 2097184 | tf_op jit(solution)/shard_map/all_to_all | solution.py:102
  270.2 6.0 %all-to-all-start.2 = ((bf16[64,16,1024]{2,1,0:T(8,128)(2,1)}), bf16[64,16,1024]{2,1,0:T(8,128)(2,1)}, u32[]{:S(2)}, u32[]{:S(2)}) async-start(bf16[64,16,1024]{2,1,0:T(8,128)(2,1)} %bitcast.61), calls=%async_computation.3 | async-start | bytes 4194304 | tf_op jit(solution)/shard_map/all_to_all | solution.py:99
  276.2 1.3 fusion.14
  277.5 49.9 %all-to-all-done.2 = bf16[64,16,1024]{2,1,0:T(8,128)(2,1)} async-done(((bf16[64,16,1024]{2,1,0:T(8,128)(2,1)}), bf16[64,16,1024]{2,1,0:T(8,128)(2,1)}, u32[]{:S(2)}, u32[]{:S(2)}) %all-to-all-start.2) | async-done | bytes 2097184 | tf_op jit(solution)/shard_map/all_to_all | solution.py:99
  327.4 2.9 fusion.12
  330.3 0.0 copy-done.2
  330.3 3.5 %fusion.1 = bf16[512,1024]{0,1:T(8,128)(2,1)} fusion(bf16[1024,512]{1,0:T(8,128)(2,1)} %reduce-scatter.2.cloned.1.call-done, bf16[64,16,1024]{2,1,0:T(8,128)(2,1)S(1)} %copy-done.2, pred[512,64]{0,1:T(8,128)(4,1)S(1)} %get-tuple-element.24, bf16[512,16]{0,1:T(8,128)(2,1)S(1)} %reduce_sum.84), kind=kOutput, calls=%fused_computation.6 | convolution fusion | flops 1077411840 | bytes 4243456 | tf_op jit(solution)/shard_map/dot_general | solution.py:90
  333.8 2.3 copy.30
  (11 shorter events, 0.1 us)
Async XLA Ops:
  7.2 169.3 %copy-start = (bf16[512,1024]{1,0:T(8,128)(2,1)S(1)}, bf16[512,1024]{1,0:T(8,128)(2,1)}, u32[]{:S(2)}) copy-start(bf16[512,1024]{1,0:T(8,128)(2,1)} %param.9) | copy-start | bytes 3145732
  7.2 52.1 %copy-start.4 = (bf16[128,1024]{1,0:T(8,128)(2,1)S(1)}, bf16[128,1024]{1,0:T(8,128)(2,1)}, u32[]{:S(2)}) copy-start(bf16[128,1024]{1,0:T(8,128)(2,1)} %param.11) | copy-start | bytes 786436
  61.3 6.6 %copy-start.5 = (bf16[128,1024]{1,0:T(8,128)(2,1)S(1)}, bf16[128,1024]{1,0:T(8,128)(2,1)}, u32[]{:S(2)}) copy-start(bf16[128,1024]{1,0:T(8,128)(2,1)} %param.12) | copy-start | bytes 786436
  61.3 57.8 %all-to-all-start.1 = ((bf16[64,16,1024]{2,1,0:T(8,128)(2,1)}), bf16[64,16,1024]{2,1,0:T(8,128)(2,1)S(1)}, u32[]{:S(2)}, u32[]{:S(2)}) async-start(bf16[64,16,1024]{2,1,0:T(8,128)(2,1)} %bitcast.11), calls=%async_computation.2 | async-start | bytes 4194304 | tf_op jit(solution)/shard_map/all_to_all | solution.py:76
  119.2 6.7 %copy-start.1 = (bf16[64,16,1024]{2,1,0:T(8,128)(2,1)}, bf16[64,16,1024]{2,1,0:T(8,128)(2,1)S(1)}, u32[]{:S(2)}) copy-start(bf16[64,16,1024]{2,1,0:T(8,128)(2,1)S(1)} %all-to-all-done.1) | copy-start | bytes 6291460
  119.2 6.1 %copy-start.6 = (s32[1,48]{1,0:T(1,128)S(1)}, s32[1,48]{1,0:T(1,128)}, u32[]{:S(2)}) copy-start(s32[1,48]{1,0:T(1,128)} %param.15) | copy-start | bytes 580
  119.2 57.3 %all-to-all-start = ((bf16[64,16,1024]{2,1,0:T(8,128)(2,1)}), bf16[64,16,1024]{2,1,0:T(8,128)(2,1)}, u32[]{:S(2)}, u32[]{:S(2)}) async-start(bf16[64,16,1024]{2,1,0:T(8,128)(2,1)} %bitcast.7), calls=%async_computation.1 | async-start | bytes 4194304 | tf_op jit(solution)/shard_map/all_to_all | solution.py:77
  176.5 3.0 copy-start.3
  206.7 63.5 %all-to-all-start.3 = ((bf16[64,16,1024]{2,1,0:T(8,128)(2,1)}), bf16[64,16,1024]{2,1,0:T(8,128)(2,1)S(1)}, u32[]{:S(2)}, u32[]{:S(2)}) async-start(bf16[64,16,1024]{2,1,0:T(8,128)(2,1)} %bitcast.60), calls=%async_computation.4 | async-start | bytes 4194304 | tf_op jit(solution)/shard_map/all_to_all | solution.py:102
  219.0 111.3 %reduce-scatter.2.cloned.1.call-start = ((), (), s32[]{:S(2)}) async-start(), calls=%async_computation.5 | async-start | bytes 5242880 | tf_op jit(solution)/shard_map/reduce_scatter | solution.py:121
  270.2 57.2 %all-to-all-start.2 = ((bf16[64,16,1024]{2,1,0:T(8,128)(2,1)}), bf16[64,16,1024]{2,1,0:T(8,128)(2,1)}, u32[]{:S(2)}, u32[]{:S(2)}) async-start(bf16[64,16,1024]{2,1,0:T(8,128)(2,1)} %bitcast.61), calls=%async_computation.3 | async-start | bytes 4194304 | tf_op jit(solution)/shard_map/all_to_all | solution.py:99
  277.5 52.8 %copy-start.2 = (bf16[64,16,1024]{2,1,0:T(8,128)(2,1)S(1)}, bf16[64,16,1024]{2,1,0:T(8,128)(2,1)}, u32[]{:S(2)}) copy-start(bf16[64,16,1024]{2,1,0:T(8,128)(2,1)} %copy-done.1) | copy-start | bytes 6291460
Sparse Core Ops, SparseCore 0:
  228.9 48.2 reduce-scatter.1
